TPU v7x, 32 devices: a whole 2x2x4 slice. The times are simulated.
32 devices in a mesh: layer: 8 (over z, x), land: 4 (over y, core).
Axes of the slice: x: 2, y: 2, z: 4, core: 2. Of those that a mesh axis runs over, the one named last changes fastest.
Arguments:
- gradients: bfloat16 [960, 65536], P(None, ('layer', 'land')), may hold values from -6 to 6
- queries: bfloat16 [32, 65536], P(None, ('layer', 'land')), may hold values from -6 to 6
- landmarks: bfloat16 [1024, 65536], P(None, ('layer', 'land')), may hold values from -0.0234375 to 0.0234375
- whitening: bfloat16 [1024, 1024], P(None, 'land'), may hold values from -2.5 to 2.5
Outputs:
- scores: float32 [32, 960], P('land', 'layer')
All inputs are finite; a program needn't handle non-finite values.
Results may differ from a plain program's by a relative error of at most 0.023.
Values may be sent and summed in bfloat16 or wider, within the bound.
A program may use at most 128 MiB of HBM per device.

v0:
```python
import jax
import jax.numpy as jnp
from jax import lax
from jax.sharding import PartitionSpec as P

NN = (((1,), (0,)), ((), ()))
NT = (((1,), (1,)), ((), ()))


def dot(a, b, dims):
    return lax.dot_general(a, b, dims, preferred_element_type=jnp.float32)


def local(gradients, queries, landmarks, whitening):
    half = jnp.bfloat16
    factor = landmarks.shape[0] ** (-0.5)
    partial = dot(queries, landmarks, NT).astype(half)
    query_proj = lax.psum(partial, ("layer", "land"))
    query_white = dot(query_proj, whitening, NN).astype(half)
    back = lax.psum(dot(query_white, whitening, NT).astype(half), "land")
    spread = dot(back, landmarks, NN).astype(half)
    scores = dot(spread, gradients, NT) * factor
    share = lax.psum_scatter(scores.astype(half), "layer", scatter_dimension=1, tiled=True)
    return lax.psum_scatter(share, "land", scatter_dimension=0, tiled=True).astype(jnp.float32)


def solution(mesh):
    return jax.shard_map(
        local,
        mesh=mesh,
        in_specs=(
            P(None, ("layer", "land")),
            P(None, ("layer", "land")),
            P(None, ("layer", "land")),
            P(None, "land"),
        ),
        out_specs=P("land", "layer"),
        check_vma=False,
    )
```

profile of v0, /device:TPU:0, one launch (start us, length us, event | category | flops | bytes accessed | tf_op | source)
XLA Modules:
  0.0 224.0 jit_solution(2773502246041843266)
XLA Ops:
  6.5 0.0 copy-start
  6.5 0.0 copy-start.2
  6.5 0.0 copy-start.1
  6.5 0.0 all-reduce.5.cloned.1.call-start
  6.5 4.3 %convolution_convert_fusion.2 = bf16[32,1024]{1,0:T(8,128)(2,1)} fusion(bf16[32,2048]{1,0:T(8,128)(2,1)} %param.5, bf16[1024,2048]{1,0:T(8,128)(2,1)} %param.6), kind=kOutput, calls=%fused_computation.5 | convolution fusion | flops 134250496 | bytes 4390912 | tf_op jit(solution)/shard_map/dot_general | solution.py:11
  10.8 0.0 all-reduce.5.cloned.1.call-update
  10.9 0.0 all-reduce.7.cloned.1.call-start
  10.9 122.3 %all-reduce.5.cloned.1.call-done = bf16[32,1024]{1,0:T(8,128)(2,1)} async-done(((bf16[32,1024]{1,0:T(8,128)(2,1)}), bf16[32,1024]{1,0:T(8,128)(2,1)}) %all-reduce.5.cloned.1.call-update) | async-done | bytes 65552 | tf_op jit(solution)/shard_map/psum | solution.py:18
  133.2 0.0 copy-done
  133.2 2.0 convolution_convert_fusion.1
  135.2 0.0 all-reduce.7.cloned.1.call-update
  135.2 0.0 copy-done.2
  135.2 0.6 dynamic-slice
  135.8 0.0 copy-done.1
  135.8 0.6 dynamic-slice.2
  137.6 29.8 %all-reduce.7.cloned.1.call-done = bf16[32,1024]{1,0:T(8,128)(2,1)} async-done(((bf16[32,1024]{1,0:T(8,128)(2,1)}), bf16[32,1024]{1,0:T(8,128)(2,1)}) %all-reduce.7.cloned.1.call-update) | async-done | bytes 65552 | tf_op jit(solution)/shard_map/psum | solution.py:20
  167.4 5.4 %fusion.2 = bf16[32,960]{1,0:T(8,128)(2,1)S(1)} fusion(bf16[960,2048]{1,0:T(8,128)(2,1)} %param.4, bf16[32,1024]{1,0:T(8,128)(2,1)} %all-reduce.7.cloned.1.call-done, bf16[1024,2048]{1,0:T(8,128)(2,1)} %param.6), kind=kOutput, calls=%fused_computation.3 | convolution fusion | flops 260173824 | bytes 8253440 | tf_op jit(solution)/shard_map/dot_general | solution.py:11
  172.8 37.5 %all-reduce = bf16[32,960]{1,0:T(8,128)(2,1)S(1)} all-reduce(bf16[32,960]{1,0:T(8,128)(2,1)S(1)} %fusion.2), channel_id=2, replica_groups=mesh['layer'=8,'land'=4] {'layer'}, use_global_device_ids=true, to_apply=%region_2.0.clone | all-reduce | flops 30720 | bytes 122880
  210.3 0.1 constant_dynamic-slice_fusion
  210.4 6.1 %all-reduce.1 = bf16[32,120]{1,0:T(8,128)(2,1)S(1)} all-reduce(bf16[32,120]{1,0:T(8,128)(2,1)S(1)} %constant_dynamic-slice_fusion), channel_id=3, replica_groups=mesh['layer'=8,'land'=4] {'land'}, use_global_device_ids=true, to_apply=%region_3.0.clone | all-reduce | flops 3840 | bytes 15360
  216.5 0.6 dynamic-slice_convert_fusion
Async XLA Ops:
  6.5 126.7 %copy-start = (bf16[1024,256]{1,0:T(8,128)(2,1)S(1)}, bf16[1024,256]{1,0:T(8,128)(2,1)}, u32[]{:S(2)}) copy-start(bf16[1024,256]{1,0:T(8,128)(2,1)} %param.7) | copy-start | bytes 1572868
  6.5 128.7 %copy-start.2 = (u32[32]{0:T(128)S(1)}, u32[32]{0:T(128)}, u32[]{:S(2)}) copy-start(u32[32]{0:T(128)} %constant.4) | copy-start | bytes 388
  6.5 129.3 %copy-start.1 = (u32[32]{0:T(128)S(1)}, u32[32]{0:T(128)}, u32[]{:S(2)}) copy-start(u32[32]{0:T(128)} %constant.8) | copy-start | bytes 388
  6.5 126.7 %all-reduce.5.cloned.1.call-start = ((), (), s32[]{:S(2)}) async-start(), calls=%async_computation | async-start | bytes 131072 | tf_op jit(solution)/shard_map/psum | solution.py:18
  10.9 156.6 %all-reduce.7.cloned.1.call-start = ((), (), s32[]{:S(2)}) async-start(), calls=%async_computation.1 | async-start | bytes 131072 | tf_op jit(solution)/shard_map/psum | solution.py:20
Sparse Core Ops, SparseCore 0:
  12.9 120.2 all-reduce.4
  135.5 31.8 all-reduce.6
where the time goes:
time: 224 us
  waiting for transfers between devices  152 us (68%)
  blocking collectives  43.6 us (19%)
  between operations  14.7 us (7%)
  matrix products  11.6 us (5%)
    psum x1, waiting for transfers between devices, local(): query_proj = lax.psum(partial, ('layer', 'land'))  122 us
    unnamed x2, blocking collectives  43.6 us
    psum x1, waiting for transfers between devices, local(): back = lax.psum(dot(query_white, whitening, NT).astype(half), 'land')  29.8 us
    dot_general x3, matrix products, dot(): return lax.dot_general(a, b, dims, preferred_element_type=jnp.float32)  11.6 us
  transfers between devices with their start and end apart: 2, of which 2 were waited for; matrix products, arithmetic and copies ran while one was open for 1% of the time, Pallas kernels for 0%

commit v1 on v0

--- a/solution.py
+++ b/solution.py
@@ -17,7 +17,7 @@
     partial = dot(queries, landmarks, NT).astype(half)
     query_proj = lax.psum(partial, ("layer", "land"))
     query_white = dot(query_proj, whitening, NN).astype(half)
-    back = lax.psum(dot(query_white, whitening, NT).astype(half), "land")
+    back = jnp.sum(lax.all_gather(dot(query_white, whitening, NT).astype(half), "land"), axis=0)
     spread = dot(back, landmarks, NN).astype(half)
     scores = dot(spread, gradients, NT) * factor
     share = lax.psum_scatter(scores.astype(half), "layer", scatter_dimension=1, tiled=True)

time: 224 us -> 197 us (0.88)
  waiting for transfers between devices: 152 us -> 120 us
  blocking collectives: 43.6 us -> 49.6 us
    psum x1 -> x0, waiting for transfers between devices: 29.8 us -> none  [local(): back = lax.psum(dot(query_white, whitening, NT).astype(half), 'land')]
    all_gather x0 -> x1, blocking collectives: none -> 7.13 us  [local(): lax.all_gather(dot(query_white, whitening, NT).astype(half), 'land')]
    psum x1, waiting for transfers between devices: 122 us -> 120 us  [local(): query_proj = lax.psum(partial, ('layer', 'land'))]
  transfers between devices with their start and end apart: 2 -> 1, of which waited for: 2 -> 1; matrix products, arithmetic and copies ran while one was open for 1% -> 1% of each run, Pallas kernels for 0% -> 0%
where the time goes in v1:
time: 197 us
  waiting for transfers between devices  120 us (61%)
  blocking collectives  49.6 us (25%)
  between operations  14.6 us (7%)
  matrix products  10.9 us (6%)
    psum x1, waiting for transfers between devices, local(): query_proj = lax.psum(partial, ('layer', 'land'))  120 us
    unnamed x2, blocking collectives  42.5 us
    dot_general x3, matrix products, dot(): return lax.dot_general(a, b, dims, preferred_element_type=jnp.float32)  10.9 us
    all_gather x1, blocking collectives, local(): lax.all_gather(dot(query_white, whitening, NT).astype(half), 'land')  7.13 us
  transfers between devices with their start and end apart: 1, of which 1 were waited for; matrix products, arithmetic and copies ran while one was open for 1% of the time, Pallas kernels for 0%

profile of v1, /device:TPU:0, one launch (start us, length us, event | category | flops | bytes accessed | tf_op | source)
XLA Modules:
  0.0 197.1 jit_solution(12049667483593894838)
XLA Ops:
  6.5 0.0 copy-start
  6.5 0.0 copy-start.2
  6.5 0.0 copy-start.1
  6.5 0.0 all-reduce.4.cloned.1.call-start
  6.5 4.3 %convolution_convert_fusion.2 = bf16[32,1024]{1,0:T(8,128)(2,1)} fusion(bf16[32,2048]{1,0:T(8,128)(2,1)} %param.5, bf16[1024,2048]{1,0:T(8,128)(2,1)} %param.6), kind=kOutput, calls=%fused_computation.5 | convolution fusion | flops 134250496 | bytes 4390912 | tf_op jit(solution)/shard_map/dot_general | solution.py:11
  10.8 0.0 all-reduce.4.cloned.1.call-update
  10.9 0.0 copy-done.2
  10.9 0.6 dynamic-slice
  11.4 0.0 copy-done.1
  11.5 0.6 dynamic-slice.2
  13.2 120.0 %all-reduce.4.cloned.1.call-done = bf16[32,1024]{1,0:T(8,128)(2,1)} async-done(((bf16[32,1024]{1,0:T(8,128)(2,1)}), bf16[32,1024]{1,0:T(8,128)(2,1)}) %all-reduce.4.cloned.1.call-update) | async-done | bytes 65552 | tf_op jit(solution)/shard_map/psum | solution.py:18
  133.2 0.0 copy-done
  133.2 1.3 convolution_convert_fusion.1
  134.5 7.1 %all-gather = bf16[128,1024]{1,0:T(8,128)(2,1)S(1)} all-gather(bf16[32,1024]{1,0:T(8,128)(2,1)S(1)} %convolution_convert_fusion.1), channel_id=2, replica_groups=mesh['layer'=8,'land'=4] {'land'}, dimensions={0}, use_global_device_ids=true | all-gather | bytes 327680 | tf_op jit(solution)/shard_map/all_gather | solution.py:20
  141.7 5.3 %fusion.2 = bf16[32,960]{1,0:T(8,128)(2,1)S(1)} fusion(bf16[960,2048]{1,0:T(8,128)(2,1)} %param.4, bf16[32,1024]{1,0:T(8,128)(2,1)S(1)} %reduce_sum.12, bf16[1024,2048]{1,0:T(8,128)(2,1)} %param.6), kind=kOutput, calls=%fused_computation.3 | convolution fusion | flops 260173824 | bytes 8253440 | tf_op jit(solution)/shard_map/dot_general | solution.py:11
  147.1 36.4 %all-reduce = bf16[32,960]{1,0:T(8,128)(2,1)S(1)} all-reduce(bf16[32,960]{1,0:T(8,128)(2,1)S(1)} %fusion.2), channel_id=3, replica_groups=mesh['layer'=8,'land'=4] {'layer'}, use_global_device_ids=true, to_apply=%region_2.0.clone | all-reduce | flops 30720 | bytes 122880
  183.5 0.1 constant_dynamic-slice_fusion
  183.6 6.1 %all-reduce.1 = bf16[32,120]{1,0:T(8,128)(2,1)S(1)} all-reduce(bf16[32,120]{1,0:T(8,128)(2,1)S(1)} %constant_dynamic-slice_fusion), channel_id=4, replica_groups=mesh['layer'=8,'land'=4] {'land'}, use_global_device_ids=true, to_apply=%region_3.0.clone | all-reduce | flops 3840 | bytes 15360
  189.6 0.6 dynamic-slice_convert_fusion
  (1 shorter events, 0.0 us)
Async XLA Ops:
  6.5 126.7 %copy-start = (bf16[1024,256]{1,0:T(8,128)(2,1)S(1)}, bf16[1024,256]{1,0:T(8,128)(2,1)}, u32[]{:S(2)}) copy-start(bf16[1024,256]{1,0:T(8,128)(2,1)} %param.7) | copy-start | bytes 1572868
  6.5 4.3 %copy-start.2 = (u32[32]{0:T(128)S(1)}, u32[32]{0:T(128)}, u32[]{:S(2)}) copy-start(u32[32]{0:T(128)} %constant.7) | copy-start | bytes 388
  6.5 4.9 %copy-start.1 = (u32[32]{0:T(128)S(1)}, u32[32]{0:T(128)}, u32[]{:S(2)}) copy-start(u32[32]{0:T(128)} %constant.11) | copy-start | bytes 388
  6.5 126.7 %all-reduce.4.cloned.1.call-start = ((), (), s32[]{:S(2)}) async-start(), calls=%async_computation | async-start | bytes 131072 | tf_op jit(solution)/shard_map/psum | solution.py:18
Sparse Core Ops, SparseCore 0:
  12.9 120.2 all-reduce.3

commit v2 on v0

--- a/solution.py
+++ b/solution.py
@@ -15,7 +15,7 @@
     half = jnp.bfloat16
     factor = landmarks.shape[0] ** (-0.5)
     partial = dot(queries, landmarks, NT).astype(half)
-    query_proj = lax.psum(partial, ("layer", "land"))
+    query_proj = lax.psum(lax.psum(partial, "land"), "layer")
     query_white = dot(query_proj, whitening, NN).astype(half)
     back = lax.psum(dot(query_white, whitening, NT).astype(half), "land")
     spread = dot(back, landmarks, NN).astype(half)

time: 224 us -> 207 us (0.924)
  waiting for transfers between devices: 152 us -> 135 us
    psum x1 -> x2, waiting for transfers between devices: 122 us -> 106 us  [local(): query_proj = lax.psum(lax.psum(partial, 'land'), 'layer')]
  transfers between devices with their start and end apart: 2 -> 3, of which waited for: 2 -> 3; matrix products, arithmetic and copies ran while one was open for 1% -> 1% of each run, Pallas kernels for 0% -> 0%
where the time goes in v2:
time: 207 us
  waiting for transfers between devices  135 us (65%)
  blocking collectives  43.6 us (21%)
  between operations  14.4 us (7%)
  matrix products  11.6 us (6%)
    psum x2, waiting for transfers between devices, local(): query_proj = lax.psum(lax.psum(partial, 'land'), 'layer')  106 us
    unnamed x2, blocking collectives  43.6 us
    psum x1, waiting for transfers between devices, local(): back = lax.psum(dot(query_white, whitening, NT).astype(half), 'land')  29.1 us
    dot_general x3, matrix products, dot(): return lax.dot_general(a, b, dims, preferred_element_type=jnp.float32)  11.6 us
  transfers between devices with their start and end apart: 3, of which 3 were waited for; matrix products, arithmetic and copies ran while one was open for 1% of the time, Pallas kernels for 0%

profile of v2, /device:TPU:0, one launch (start us, length us, event | category | flops | bytes accessed | tf_op | source)
XLA Modules:
  0.0 206.8 jit_solution(174283497223842191)
XLA Ops:
  6.5 0.0 copy-start
  6.5 0.0 copy-start.2
  6.5 0.0 copy-start.1
  6.5 0.0 all-reduce.6.cloned.1.call-start
  6.5 4.3 %convolution_convert_fusion.2 = bf16[32,1024]{1,0:T(8,128)(2,1)} fusion(bf16[32,2048]{1,0:T(8,128)(2,1)} %param.5, bf16[1024,2048]{1,0:T(8,128)(2,1)} %param.6), kind=kOutput, calls=%fused_computation.5 | convolution fusion | flops 134250496 | bytes 4390912 | tf_op jit(solution)/shard_map/dot_general | solution.py:11
  10.8 0.0 all-reduce.6.cloned.1.call-update
  10.8 0.0 all-reduce.8.cloned.1.call-start
  10.9 33.8 %all-reduce.6.cloned.1.call-done = bf16[32,1024]{1,0:T(8,128)(2,1)} async-done(((bf16[32,1024]{1,0:T(8,128)(2,1)}), bf16[32,1024]{1,0:T(8,128)(2,1)}) %all-reduce.6.cloned.1.call-update) | async-done | bytes 65552 | tf_op jit(solution)/shard_map/psum | solution.py:18
  44.7 0.0 all-reduce.8.cloned.1.call-update
  44.8 0.0 all-reduce.10.cloned.1.call-start
  44.8 72.2 %all-reduce.8.cloned.1.call-done = bf16[32,1024]{1,0:T(8,128)(2,1)} async-done(((bf16[32,1024]{1,0:T(8,128)(2,1)}), bf16[32,1024]{1,0:T(8,128)(2,1)}) %all-reduce.8.cloned.1.call-update) | async-done | bytes 65552 | tf_op jit(solution)/shard_map/psum | solution.py:18
  117.1 0.0 copy-done
  117.1 2.0 convolution_convert_fusion.1
  119.0 0.0 all-reduce.10.cloned.1.call-update
  119.1 0.0 copy-done.2
  119.1 0.6 dynamic-slice
  119.7 0.0 copy-done.1
  119.7 0.6 dynamic-slice.2
  121.5 29.1 %all-reduce.10.cloned.1.call-done = bf16[32,1024]{1,0:T(8,128)(2,1)} async-done(((bf16[32,1024]{1,0:T(8,128)(2,1)}), bf16[32,1024]{1,0:T(8,128)(2,1)}) %all-reduce.10.cloned.1.call-update) | async-done | bytes 65552 | tf_op jit(solution)/shard_map/psum | solution.py:20
  150.5 5.4 %fusion.2 = bf16[32,960]{1,0:T(8,128)(2,1)S(1)} fusion(bf16[960,2048]{1,0:T(8,128)(2,1)} %param.4, bf16[32,1024]{1,0:T(8,128)(2,1)} %all-reduce.10.cloned.1.call-done, bf16[1024,2048]{1,0:T(8,128)(2,1)} %param.6), kind=kOutput, calls=%fused_computation.3 | convolution fusion | flops 260173824 | bytes 8253440 | tf_op jit(solution)/shard_map/dot_general | solution.py:11
  155.9 37.5 %all-reduce = bf16[32,960]{1,0:T(8,128)(2,1)S(1)} all-reduce(bf16[32,960]{1,0:T(8,128)(2,1)S(1)} %fusion.2), channel_id=2, replica_groups=mesh['layer'=8,'land'=4] {'layer'}, use_global_device_ids=true, to_apply=%region_3.0.clone | all-reduce | flops 30720 | bytes 122880
  193.4 0.1 constant_dynamic-slice_fusion
  193.5 6.1 %all-reduce.1 = bf16[32,120]{1,0:T(8,128)(2,1)S(1)} all-reduce(bf16[32,120]{1,0:T(8,128)(2,1)S(1)} %constant_dynamic-slice_fusion), channel_id=3, replica_groups=mesh['layer'=8,'land'=4] {'land'}, use_global_device_ids=true, to_apply=%region_4.0.clone | all-reduce | flops 3840 | bytes 15360
  199.6 0.6 dynamic-slice_convert_fusion
Async XLA Ops:
  6.5 110.5 %copy-start = (bf16[1024,256]{1,0:T(8,128)(2,1)S(1)}, bf16[1024,256]{1,0:T(8,128)(2,1)}, u32[]{:S(2)}) copy-start(bf16[1024,256]{1,0:T(8,128)(2,1)} %param.7) | copy-start | bytes 1572868
  6.5 112.5 %copy-start.2 = (u32[32]{0:T(128)S(1)}, u32[32]{0:T(128)}, u32[]{:S(2)}) copy-start(u32[32]{0:T(128)} %constant.4) | copy-start | bytes 388
  6.5 113.1 %copy-start.1 = (u32[32]{0:T(128)S(1)}, u32[32]{0:T(128)}, u32[]{:S(2)}) copy-start(u32[32]{0:T(128)} %constant.8) | copy-start | bytes 388
  6.5 38.2 %all-reduce.6.cloned.1.call-start = ((), (), s32[]{:S(2)}) async-start(), calls=%async_computation | async-start | bytes 131072 | tf_op jit(solution)/shard_map/psum | solution.py:18
  10.8 106.2 %all-reduce.8.cloned.1.call-start = ((), (), s32[]{:S(2)}) async-start(), calls=%async_computation.1 | async-start | bytes 131072 | tf_op jit(solution)/shard_map/psum | solution.py:18
  44.8 105.8 %all-reduce.10.cloned.1.call-start = ((), (), s32[]{:S(2)}) async-start(), calls=%async_computation.2 | async-start | bytes 131072 | tf_op jit(solution)/shard_map/psum | solution.py:20
Sparse Core Ops, SparseCore 0:
  11.0 33.7 all-reduce.5
  48.5 68.4 all-reduce.7
  119.5 30.9 all-reduce.9
